TPU v7x, 32 devices: a whole 2x2x4 slice. The times are simulated.
32 devices in a mesh: frames: 8 (over y, x, core), expert: 4 (over z).
Axes of the slice: x: 2, y: 2, z: 4, core: 2. Of those that a mesh axis runs over, the one named last changes fastest.
Arguments:
- residual: bfloat16 [8, 512, 1152], P('frames', 'expert'), may hold values from -6 to 6
- queries: bfloat16 [8, 512, 1152], P('frames', 'expert'), may hold values from -8 to 8
- keys_in: bfloat16 [8, 512, 1152], P('frames', 'expert'), may hold values from -8 to 8
- values: bfloat16 [8, 512, 1152], P('frames', 'expert'), may hold values from -6 to 6
- w_out: bfloat16 [1152, 1152], replicated, may hold values from -0.1875 to 0.1875
- norm_gain: float32 [1152], replicated, may hold values from 0.5 to 2
- w_router: bfloat16 [1152, 16], replicated, may hold values from -0.1875 to 0.1875
- routes: int32 [4, 8, 128, 2], P('expert', 'frames'), may hold values from 0 to 15, all different within a row; in each aligned block of 128 rows (0 to 127, 128 to 255, ..., all dimensions but the last counted through in order) at most 32 rows name the same one
- w_gate: bfloat16 [32, 1152, 512], P(('frames', 'expert')), may hold values from -0.1875 to 0.1875
- w_up: bfloat16 [32, 1152, 512], P(('frames', 'expert')), may hold values from -0.1875 to 0.1875
- w_down: bfloat16 [32, 512, 1152], P(('frames', 'expert')), may hold values from -0.1875 to 0.1875
- d_out: bfloat16 [8, 512, 1152], P('frames', 'expert'), may hold values from -2 to 2
Outputs:
- block_out: bfloat16 [8, 512, 1152], P('frames', 'expert')
- d_hidden: bfloat16 [8, 512, 1152], P('frames', 'expert')
- d_gate: float32 [32, 1152, 512], P(('frames', 'expert'))
- d_up: float32 [32, 1152, 512], P(('frames', 'expert'))
- d_down: float32 [32, 512, 1152], P(('frames', 'expert'))
Inputs may be any that keep to these rules, and one draw needn't show every extreme that they name: `routes`: the two experts of a token differ. In the rows of one device (the aligned blocks of 128 rows over the flattened leading dimensions) no expert is named more than 32 times; some expert is named exactly 32 times in some of these blocks.
All inputs are finite; a program needn't handle non-finite values.
Results may differ from a plain program's by a relative error of at most 0.018.
Values may be sent and summed in bfloat16 or wider, within the bound.
A program may use at most 128 MiB of HBM per device.

v0:
```python
import functools

import jax
import jax.numpy as jnp
from jax import lax
from jax.experimental import pallas as pl
from jax.experimental.pallas import tpu as pltpu
from jax.sharding import PartitionSpec as P

H = 16
LANES = 128
VM = pltpu.VMEM
BF = jnp.bfloat16
F32 = jnp.float32


def head_windows(width):
    head = width // H
    for h in range(H):
        lo, hi = h * head, (h + 1) * head
        yield lo, hi, lo // LANES * LANES, -(-hi // LANES) * LANES


def attend(q, k, v, out, acc, positions):
    rows, width = q.shape
    scale = (width // H) ** (-0.5)
    at = lax.broadcasted_iota(jnp.int32, (rows, rows), 0) % positions
    other = lax.broadcasted_iota(jnp.int32, (rows, rows), 1) % positions
    same = at == other
    acc[...] = jnp.zeros(acc.shape, F32)
    for lo, hi, w0, w1 in head_windows(width):
        lane = lax.broadcasted_iota(jnp.int32, (rows, w1 - w0), 1) + w0
        mine = (lane >= lo) & (lane < hi)
        zero = jnp.zeros((rows, w1 - w0), BF)
        qh = jnp.where(mine, q[:, w0:w1], zero)
        scores = (
            lax.dot_general(qh, k[:, w0:w1], (((1,), (1,)), ((), ())), preferred_element_type=F32)
            * scale
        )
        scores = jnp.where(same, scores, -1e30)
        weights = jnp.exp(scores - jnp.max(scores, axis=-1, keepdims=True))
        probs = (weights / jnp.sum(weights, axis=-1, keepdims=True)).astype(BF)
        vh = jnp.where(mine, v[:, w0:w1], zero)
        acc[:, w0:w1] += jnp.dot(probs, vh, preferred_element_type=F32)
    out[...] = acc[...].astype(BF)


def attention(q, k, v, positions):
    def body(q_ref, k_ref, v_ref, out_ref, acc):
        attend(q_ref, k_ref, v_ref, out_ref, acc, positions)

    return pl.pallas_call(
        body,
        out_shape=jax.ShapeDtypeStruct(q.shape, BF),
        scratch_shapes=[VM(q.shape, F32)],
    )(q, k, v)


def dot(a, b, ca, cb):
    return lax.dot_general(a, b, (((ca,), (cb,)), ((), ())), preferred_element_type=F32)


def expert_body(x, cot, router, gate, up, down, y, r, d_gate, d_up, d_down):
    xv, cv = x[...], cot[...]
    wr = router[...].astype(F32)
    logit = jnp.sum(xv.astype(F32) * wr, axis=-1, keepdims=True)
    combine = jax.nn.sigmoid(logit)
    cf = cv.astype(F32)
    scaled = (combine * cf).astype(BF)
    pre_gate = dot(xv, gate[...], 1, 0)
    pre_up = dot(xv, up[...], 1, 0)
    sig = jax.nn.sigmoid(pre_gate)
    act = pre_gate * sig
    units = (act * pre_up).astype(BF)
    part = dot(units, down[...], 1, 0).astype(BF).astype(F32)
    y[...] = (combine * part).astype(BF)
    d_units = dot(scaled, down[...], 1, 1)
    dpg = (d_units * pre_up * (sig + act * (1.0 - sig))).astype(BF)
    dpu = (d_units * act).astype(BF)
    d_logit = jnp.sum(cf * part, axis=-1, keepdims=True) * combine * (1.0 - combine)
    d_in = dot(dpg, gate[...], 1, 1) + dot(dpu, up[...], 1, 1)
    r[...] = (d_in + d_logit * wr).astype(BF)
    first = pl.program_id(0) == 0

    @pl.when(first)
    def _():
        d_gate[...] = dot(xv, dpg, 0, 0)
        d_up[...] = dot(xv, dpu, 0, 0)
        d_down[...] = dot(units, scaled, 0, 0)

    @pl.when(jnp.logical_not(first))
    def _():
        d_gate[...] += dot(xv, dpg, 0, 0)
        d_up[...] += dot(xv, dpu, 0, 0)
        d_down[...] += dot(units, scaled, 0, 0)


def expert(x, cot, router, gate, up, down):
    slots, width = x.shape
    hidden = gate.shape[1]
    block = 256 if slots % 256 == 0 else slots
    rows = pl.BlockSpec((block, width), lambda i: (i, 0))

    def whole(shape):
        return pl.BlockSpec(shape, lambda i: (0, 0))

    return pl.pallas_call(
        expert_body,
        grid=(slots // block,),
        in_specs=[rows, rows, whole((1, width)), whole(gate.shape), whole(up.shape), whole(down.shape)],
        out_specs=[rows, rows, whole(gate.shape), whole(up.shape), whole(down.shape)],
        out_shape=[
            jax.ShapeDtypeStruct(x.shape, BF),
            jax.ShapeDtypeStruct(x.shape, BF),
            jax.ShapeDtypeStruct(gate.shape, F32),
            jax.ShapeDtypeStruct(up.shape, F32),
            jax.ShapeDtypeStruct(down.shape, F32),
        ],
        compiler_params=pltpu.CompilerParams(vmem_limit_bytes=60 * 2**20),
    )(x, cot, router, gate, up, down)


def picker(routes_z, expert_count, capacity, frames, depth, z):
    groups, tokens, _ = routes_z.shape
    ids = jnp.arange(expert_count, dtype=jnp.int32)
    onehot = (routes_z[:, :, :, None] == ids).astype(F32).sum(axis=2)
    tri = (jnp.arange(tokens)[:, None] > jnp.arange(tokens)[None, :]).astype(BF)
    before = jnp.einsum("ts,gse->gte", tri, onehot.astype(BF), preferred_element_type=F32)
    mine = frames * depth // 2 // (depth // 2)
    own = (jnp.arange(mine) * (depth // 2)) + z // 2
    hot = jnp.take(onehot, own, axis=2)
    rank = jnp.take(before, own, axis=2)
    place = jnp.where(hot > 0, rank, -1.0).transpose(0, 2, 1)
    slot = jnp.arange(capacity, dtype=F32)
    return (place[:, :, None, :] == slot[None, None, :, None]).astype(BF).reshape(
        groups, mine * capacity, tokens
    )


MESH = pl.DeviceIdType.MESH
ANY = pl.BlockSpec(memory_space=pl.ANY)


def remote(src, dst, send, recv, **to):
    return pltpu.make_async_remote_copy(
        src_ref=src, dst_ref=dst, send_sem=send, recv_sem=recv, device_id=to, device_id_type=MESH
    )


def each_peer(frames, f, fn):
    def step(o, carry):
        fn(o, lax.rem(f + o, frames), lax.rem(f + frames - o, frames))
        return carry

    lax.fori_loop(1, frames, step, 0)


def greet(frames, depth, f, z):
    barrier = pltpu.get_barrier_semaphore()
    for o in range(1, frames):
        pl.semaphore_signal(
            barrier, inc=1, device_id={"frames": lax.rem(f + o, frames)}, device_id_type=MESH
        )
    for o in range(1, depth):
        pl.semaphore_signal(
            barrier, inc=1, device_id={"expert": lax.rem(z + o, depth)}, device_id_type=MESH
        )
    pl.semaphore_wait(barrier, frames + depth - 2)


def turn(k, z):
    if isinstance(k, int):
        return (z, z + 1 - 2 * (z % 2), 2 - z // 2, 3 - 3 * (z // 2))[k]
    near = jnp.where(k == 0, turn(0, z), turn(1, z))
    return jnp.where(k < 2, near, jnp.where(k == 2, turn(2, z), turn(3, z)))


class Relay:
    def __init__(self, depth, z, held, send, recv):
        self.depth, self.z, self.held, self.send, self.recv = depth, z, held, send, recv

    def hop(self, b, up):
        to = jnp.minimum(self.z + 1, self.depth - 1) if up else jnp.maximum(self.z - 1, 0)
        return remote(
            self.held.at[b], self.held.at[b], self.send.at[int(up), b], self.recv.at[b], expert=to
        )

    def pass_on(self, b, fn):
        @pl.when((b <= self.z) & (self.z < self.depth - 1))
        def _():
            fn(self.hop(b, True))

        @pl.when((b >= self.z) & (self.z > 0))
        def _():
            fn(self.hop(b, False))

    def start(self, b):
        self.pass_on(b, lambda c: c.start())

    def arrive(self, b):
        self.hop(b, True).wait_recv()

    def finish(self):
        for b in range(self.depth):
            self.pass_on(b, lambda c: c.wait_send())


def pick_rows(pick, block, frames):
    rows = jnp.dot(pick, block, preferred_element_type=F32).astype(BF)
    return rows.reshape(frames, rows.shape[0] // frames, rows.shape[1])


def tail_body(
    hidden_in, sums_in, d_out_in, gain, g0, g1, g2, block_out, d_hidden, o0, o1, o2,
    hidden, sums, d_out, b0, b1, b2, w0, w1, w2, ls, ins, outs,
):
    small = [
        pltpu.make_async_copy(src, dst, ls.at[i])
        for i, (src, dst) in enumerate(((hidden_in, hidden), (sums_in, sums), (d_out_in, d_out)))
    ]
    for c in small:
        c.start()
    steps = []
    for i, (src, buf, wide, dst) in enumerate(
        ((g0, b0, w0, o0), (g1, b1, w1, o1), (g2, b2, w2, o2))
    ):
        half = src.shape[0] // 2
        for j in range(2):
            at = pl.ds(j * half, half)
            steps.append(
                (
                    pltpu.make_async_copy(src.at[at], buf.at[at], ins.at[i, j]),
                    pltpu.make_async_copy(wide.at[at], dst.at[at], outs.at[i, j]),
                    buf.at[at],
                    wide.at[at],
                )
            )
    for fetch, *_ in steps:
        fetch.start()
    for fetch, put, narrow, wide in steps:
        fetch.wait()
        wide[...] = narrow[...].astype(F32)
        put.start()
    for c in small:
        c.wait()
    hf = hidden[...].astype(F32)
    inv = lax.rsqrt(jnp.mean(hf * hf, axis=-1, keepdims=True) + 1e-06)
    block_out[...] = (hf + sums[0]).astype(BF)
    gained = sums[1] * gain[...].reshape(1, hf.shape[1])
    d_norm_in = inv * gained - hf * (inv * inv * inv) * jnp.mean(gained * hf, axis=-1, keepdims=True)
    d_hidden[...] = (d_out[...].astype(F32) + d_norm_in).astype(BF)
    for _, put, *_ in steps:
        put.wait()


def tail(hidden, sums, d_out, gain, grads):
    vm = pl.BlockSpec(memory_space=VM)
    dma = pltpu.SemaphoreType.DMA
    return pl.pallas_call(
        tail_body,
        in_specs=[ANY] * 3 + [vm] + [ANY] * 3,
        out_specs=[vm, vm, ANY, ANY, ANY],
        out_shape=[jax.ShapeDtypeStruct(hidden.shape, BF)] * 2
        + [jax.ShapeDtypeStruct(g.shape, F32) for g in grads],
        scratch_shapes=[VM(t.shape, t.dtype) for t in (hidden, sums, d_out, *grads)]
        + [VM(g.shape, F32) for g in grads]
        + [dma((3,)), dma((3, 2)), dma((3, 2))],
        compiler_params=pltpu.CompilerParams(vmem_limit_bytes=60 * 2**20),
    )(hidden, sums, d_out, gain, *grads)


def fused_body(
    frames, depth, q, k, v, d_out, routes, residual, w_out, gain, router, gate_in, up_in, down_in,
    hidden, sums, gate_out, up_out, down_out,
    d_gate, d_up, d_down, n_gate, n_up, n_down, proj, column, qkv, flat, acc, mix, att, place, pick, held_d, held, cot_slots, out_slots, x, cots,
    gate, up, down, yr, back, part, swapped, merged, near, far,
    qs, qr, ats, atr, ps, pr, ds, dr, zs, zr, cs, cr, xs, xr, ys, yr_sem, nsem, psem, fsem, ls,
):
    f, z = lax.axis_index("frames"), lax.axis_index("expert")
    _, positions, width = q.shape
    _, _, capacity, _ = x.shape
    tokens = frames * positions
    slots = frames * capacity
    halves = depth // 2
    par = z % 2
    partner = z + 1 - 2 * par
    loads = [
        pltpu.make_async_copy(src, dst, ls.at[i])
        for i, (src, dst) in enumerate(((gate_in, gate), (up_in, up), (down_in, down)))
    ]
    saves = [
        pltpu.make_async_copy(src, dst, ls.at[3 + i])
        for i, (src, dst) in enumerate(((n_gate, gate_out), (n_up, up_out), (n_down, down_out)))
    ]
    project = pltpu.make_async_copy(w_out, proj, ls.at[6])
    project.start()
    held_d[z] = d_out[...]
    rows = lax.broadcasted_iota(jnp.int32, (halves * frames, tokens), 0)
    ids = (rows % frames) * halves + rows // frames
    hot = (routes[0:1, :] == ids) | (routes[1:2, :] == ids)
    earlier = lax.broadcasted_iota(jnp.int32, (tokens, tokens), 0)
    later = lax.broadcasted_iota(jnp.int32, (tokens, tokens), 1)
    before = jnp.dot(
        jnp.where(hot, 1.0, 0.0).astype(BF),
        jnp.where(earlier < later, 1.0, 0.0).astype(BF),
        preferred_element_type=F32,
    )
    place[z] = jnp.where(hot, before, -1.0).reshape(halves, frames, tokens)
    greet(frames, depth, f, z)

    def exchange(fn, o, to, source):
        for i, t in enumerate((q, k, v)):
            fn(remote(t.at[to], qkv.at[i, source], qs.at[i, o], qr.at[i, o], frames=to))

    def place_copy(o, source):
        return remote(
            place.at[source], place.at[source], ps.at[o], pr.at[o], expert=lax.rem(z + o, depth)
        )

    for o in range(1, depth):
        place_copy(o, z).start()
    each_peer(frames, f, lambda o, to, fr: exchange(lambda c: c.start(), o, to, f))
    relay_d = Relay(depth, z, held_d, ds, dr)
    relay_d.start(z)
    for c in loads:
        c.start()
    expert_ids = lax.broadcasted_iota(jnp.int32, router.shape, 0)
    owned = expert_ids == (f * depth + z) // 2
    column[...] = jnp.sum(jnp.where(owned, router[...].astype(F32), 0.0), axis=0, keepdims=True)
    for i, t in enumerate((q, k, v)):
        qkv[i, f] = t[f]
    d_gate[...] = jnp.zeros(d_gate.shape, F32)
    d_up[...] = jnp.zeros(d_up.shape, F32)
    d_down[...] = jnp.zeros(d_down.shape, F32)
    for o in range(1, depth):
        place_copy(o, lax.rem(z + depth - o, depth)).wait_recv()
    slot = lax.broadcasted_iota(jnp.int32, (capacity, tokens), 0).astype(F32)
    for b in range(depth):
        at = place[b, z // halves]
        for g in range(frames):
            pick[b, g * capacity : (g + 1) * capacity, :] = jnp.where(
                at[g : g + 1, :] == slot, 1.0, 0.0
            ).astype(BF)

    def cot_copy(n, o, to, source):
        b = turn(n, z)
        return remote(cot_slots.at[b, to], cots.at[b, source], cs.at[n, o], cr.at[n, o], frames=to)

    def send_cot(n):
        b = turn(n, z)
        if n:
            relay_d.arrive(b)
            relay_d.start(b)
        cot_slots[b] = pick_rows(pick[b], held_d[b], frames)
        each_peer(frames, f, lambda o, to, fr: cot_copy(n, o, to, f).start())
        cots[b, f] = cot_slots[b, f]

    each_peer(frames, f, lambda o, to, fr: exchange(lambda c: c.wait_recv(), o, to, fr))
    send_cot(0)
    for i in range(3):
        flat[i] = qkv[i].reshape(tokens, width)
    attend(flat.at[0], flat.at[1], flat.at[2], flat.at[3], acc, positions)
    mix[...] = flat[3].reshape(frames, positions, width)

    def home(o, to, source):
        return remote(mix.at[to], att.at[source], ats.at[o], atr.at[o], frames=to)

    each_peer(frames, f, lambda o, to, fr: home(o, to, f).start())
    att[f] = mix[f]
    for n in range(1, depth):
        send_cot(n)
    each_peer(frames, f, lambda o, to, fr: home(o, to, fr).wait_recv())
    project.wait()
    stream = residual[...].astype(F32) + jnp.dot(
        att[...].reshape(tokens, width), proj[...], preferred_element_type=F32
    )
    hid = stream.astype(BF)
    hidden[...] = hid
    hf = hid.astype(F32)
    inv = lax.rsqrt(jnp.mean(hf * hf, axis=-1, keepdims=True) + 1e-06)
    held[z] = (hf * inv * gain[...].reshape(1, width)).astype(BF)

    relay = Relay(depth, z, held, zs, zr)
    relay.start(z)

    def slot_copy(n, o, to, source):
        b = turn(n, z)
        return remote(out_slots.at[b, to], x.at[b, source], xs.at[n, o], xr.at[n, o], frames=to)

    def send_slots(n):
        b = turn(n, z)
        if not (isinstance(n, int) and n == 0):
            relay.arrive(b)
            relay.start(b)
        out_slots[b] = pick_rows(pick[b], held[b], frames)
        each_peer(frames, f, lambda o, to, fr: slot_copy(n, o, to, f).start())
        x[b, f] = out_slots[b, f]

    def result_copy(n, o, to, source):
        b = turn(n, z)
        return remote(yr.at[b, to], back.at[b, source], ys.at[n, o], yr_sem.at[n, o], frames=to)

    def compute(n):
        b = turn(n, z)
        each_peer(frames, f, lambda o, to, fr: slot_copy(n, o, to, fr).wait_recv())
        each_peer(frames, f, lambda o, to, fr: cot_copy(n, o, to, fr).wait_recv())
        xv = x[b].reshape(slots, width)
        cv = cots[b].reshape(slots, width)
        wr = column[...]
        combine = jax.nn.sigmoid(jnp.sum(xv.astype(F32) * wr, axis=-1, keepdims=True))
        cf = cv.astype(F32)
        scaled = (combine * cf).astype(BF)
        pre_gate = dot(xv, gate[...], 1, 0)
        pre_up = dot(xv, up[...], 1, 0)
        sig = jax.nn.sigmoid(pre_gate)
        act = pre_gate * sig
        units = (act * pre_up).astype(BF)
        out = dot(units, down[...], 1, 0).astype(BF).astype(F32)
        yr[b, :, 0] = (combine * out).astype(BF).reshape(frames, capacity, width)
        d_units = dot(scaled, down[...], 1, 1)
        dpg = (d_units * pre_up * (sig + act * (1.0 - sig))).astype(BF)
        dpu = (d_units * act).astype(BF)
        d_logit = jnp.sum(cf * out, axis=-1, keepdims=True) * combine * (1.0 - combine)
        d_in = dot(dpg, gate[...], 1, 1) + dot(dpu, up[...], 1, 1)
        yr[b, :, 1] = (d_in + d_logit * wr).astype(BF).reshape(frames, capacity, width)
        each_peer(frames, f, lambda o, to, fr: result_copy(n, o, to, f).start())
        back[b, f] = yr[b, f]
        d_gate[...] += dot(xv, dpg, 0, 0)
        d_up[...] += dot(xv, dpu, 0, 0)
        d_down[...] += dot(units, scaled, 0, 0)

    def totals(n):
        b = turn(n, z)
        each_peer(frames, f, lambda o, to, fr: result_copy(n, o, to, fr).wait_recv())
        for i in range(2):
            yield dot(pick[b], back[b, :, i].reshape(slots, width), 0, 0)

    def near_copy():
        return remote(part.at[1], near, nsem.at[0], nsem.at[1], expert=partner)

    def swap_copy(n):
        return remote(part.at[n, 1 - par], swapped.at[n], psem.at[0, n], psem.at[1, n], expert=partner)

    def far_copy(n):
        return remote(merged.at[n], far.at[par], fsem.at[0, n], fsem.at[1, par], expert=turn(n, z))

    def collect(n):
        for i, total in enumerate(totals(n)):
            part[n, i] = total.astype(BF)

        @pl.when(n == 1)
        def _():
            near_copy().start()

        @pl.when(n > 1)
        def _():
            swap_copy(n).start()

    def forward(n):
        swap_copy(n).wait_recv()
        merged[n] = (part[n, par].astype(F32) + swapped[n].astype(F32)).astype(BF)
        far_copy(n).start()

    for n in range(depth):
        send_slots(n)
    for c in loads:
        c.wait()

    def order(i):
        return jnp.where(i < 2, i + 2, 3 - i)

    def step(i, carry):
        compute(order(i))

        @pl.when(i > 1)
        def _():
            forward(i)

        @pl.when(i > 0)
        def _():
            collect(order(i - 1))

        return carry

    lax.fori_loop(0, depth, step, 0)
    for narrow, total in ((n_gate, d_gate), (n_up, d_up), (n_down, d_down)):
        narrow[...] = total[...].astype(BF)
    for c in saves:
        c.start()
    own = list(totals(0))
    near_copy().wait_recv()
    for i in range(2):
        arrived = remote(merged.at[2], far.at[i], fsem.at[0, 2], fsem.at[1, i], expert=partner)
        arrived.wait_recv()
        sums[i] = own[i] + near[i].astype(F32) + far[i].astype(F32)
    near_copy().wait_send()
    for n in range(2, depth):
        swap_copy(n).wait_send()
        far_copy(n).wait_send()
    for n in range(depth):
        each_peer(frames, f, lambda o, to, fr: slot_copy(n, o, to, f).wait_send())
        each_peer(frames, f, lambda o, to, fr: result_copy(n, o, to, f).wait_send())
    relay.finish()
    for c in saves:
        c.wait()
    relay_d.finish()
    for o in range(1, depth):
        place_copy(o, z).wait_send()
    for n in range(depth):
        each_peer(frames, f, lambda o, to, fr: cot_copy(n, o, to, f).wait_send())
    each_peer(frames, f, lambda o, to, fr: exchange(lambda c: c.wait_send(), o, to, f))
    each_peer(frames, f, lambda o, to, fr: home(o, to, f).wait_send())


def fused(q, k, v, d_out, routes, residual, w_out, gain, router, gate, up, down, depth, capacity):
    frames, positions, width = q.shape
    tokens = frames * positions
    dma = pltpu.SemaphoreType.DMA
    vm = pl.BlockSpec(memory_space=VM)
    slots = (depth, frames, capacity, width)
    pair = (depth, frames, 2, capacity, width)
    blocks = (depth, tokens, width)
    chunked = (frames, positions, width)
    two = (2, tokens, width)
    return pl.pallas_call(
        functools.partial(fused_body, frames, depth),
        in_specs=[vm] * 6 + [ANY, vm, vm] + [ANY] * 3,
        out_specs=[vm] * 2 + [ANY] * 3,
        out_shape=[
            jax.ShapeDtypeStruct((tokens, width), BF),
            jax.ShapeDtypeStruct(two, F32),
            jax.ShapeDtypeStruct(gate.shape, BF),
            jax.ShapeDtypeStruct(up.shape, BF),
            jax.ShapeDtypeStruct(down.shape, BF),
        ],
        scratch_shapes=[
            VM(gate.shape, F32), VM(up.shape, F32), VM(down.shape, F32),
            VM(gate.shape, BF), VM(up.shape, BF), VM(down.shape, BF), VM(w_out.shape, BF), VM((1, width), F32),
            VM((3,) + chunked, BF), VM((4, tokens, width), BF), VM((tokens, width), F32),
            VM(chunked, BF), VM(chunked, BF),
            VM((depth, depth // 2, frames, tokens), F32),
            VM((depth, frames * capacity, tokens), BF),
            VM(blocks, BF), VM(blocks, BF),
            VM(slots, BF), VM(slots, BF), VM(slots, BF), VM(slots, BF),
            VM(gate.shape, BF), VM(up.shape, BF), VM(down.shape, BF),
            VM(pair, BF), VM(pair, BF),
            VM((depth,) + two, BF), VM(blocks, BF), VM(blocks, BF), VM(two, BF), VM(two, BF),
            dma((3, frames)), dma((3, frames)), dma((frames,)), dma((frames,)),
            dma((depth,)), dma((depth,)),
            dma((2, depth)), dma((depth,)), dma((2, depth)), dma((depth,)),
            dma((depth, frames)), dma((depth, frames)), dma((depth, frames)), dma((depth, frames)),
            dma((depth, frames)), dma((depth, frames)),
            dma((2,)), dma((2, depth)), dma((2, depth)), dma((7,)),
        ],
        compiler_params=pltpu.CompilerParams(
            collective_id=0, has_side_effects=True, vmem_limit_bytes=60 * 2**20
        ),
    )(q, k, v, d_out, routes, residual, w_out, gain, router, gate, up, down)


def on_device(
    residual, queries, keys_in, values, w_out, norm_gain, w_router, routes, w_gate, w_up, w_down, d_out
):
    _, tokens, width = residual.shape
    frames, depth = lax.axis_size("frames"), lax.axis_size("expert")
    f, z = lax.axis_index("frames"), lax.axis_index("expert")
    expert_count = w_router.shape[1]
    capacity = 4 * tokens // expert_count
    positions = tokens // frames

    def across(t):
        return lax.all_to_all(
            t.reshape(frames, -1, width), "frames", split_axis=0, concat_axis=0, tiled=True
        )


    own = (f * depth + z) // 2
    router = lax.dynamic_slice(w_router, (0, own), (width, 1)).reshape(1, width)
    if positions % 16 == 0 and capacity % 16 == 0 and depth == 4:
        rows = d_out.reshape(tokens, width)
        hidden, sums, *grads = fused(
            *(t.reshape(frames, positions, width) for t in (queries, keys_in, values)),
            rows, routes.reshape(tokens, 2).T, residual.reshape(tokens, width), w_out, norm_gain,
            w_router.T, w_gate[0], w_up[0], w_down[0], depth, capacity,
        )
        block_out, d_hidden, *grads = tail(hidden, sums, rows, norm_gain, grads)
        return (
            block_out.reshape(residual.shape), d_hidden.reshape(residual.shape),
            *(g[None] for g in grads),
        )

    routes_z = lax.all_gather(routes.reshape(tokens, 2), "expert", axis=0)
    pick = picker(routes_z, expert_count, capacity, frames, depth, z)
    def dispatch(rows):
        gathered = lax.all_gather(rows, "expert", axis=0)
        picked = jnp.einsum("gst,gtd->gsd", pick, gathered, preferred_element_type=F32).astype(BF)
        picked = picked.reshape(depth, frames, capacity, width).transpose(1, 0, 2, 3)
        return across(picked).reshape(frames * depth * capacity, width)

    q, k, v = (across(t).reshape(tokens, width) for t in (queries, keys_in, values))
    cot = dispatch(d_out.reshape(tokens, width))
    attended = across(attention(q, k, v, positions)).reshape(tokens, width)
    stream = residual.reshape(tokens, width).astype(F32) + jnp.dot(
        attended, w_out, preferred_element_type=F32
    )
    hidden = stream.astype(BF)
    hidden_float = hidden.astype(F32)
    inv_rms = lax.rsqrt(jnp.mean(hidden_float * hidden_float, axis=-1, keepdims=True) + 1e-06)
    normed = (hidden_float * inv_rms * norm_gain).astype(BF)
    x = dispatch(normed)
    y, r, d_gate, d_up, d_down = expert(x, cot, router, w_gate[0], w_up[0], w_down[0])

    def collect(rows):
        back = across(rows).reshape(frames, depth, capacity, width).transpose(1, 0, 2, 3)
        back = back.reshape(depth, frames * capacity, width)
        sums = jnp.einsum("gst,gsd->gtd", pick, back, preferred_element_type=F32).astype(BF)
        return lax.psum_scatter(sums, "expert", scatter_dimension=0, tiled=True)[0].astype(F32)

    expert_sum = collect(y)
    d_normed = collect(r)
    return finish(
        residual, d_out, norm_gain, hidden_float, inv_rms, expert_sum, d_normed, d_gate, d_up, d_down
    )


def finish(
    residual, d_out, norm_gain, hidden_float, inv_rms, expert_sum, d_normed, d_gate, d_up, d_down
):
    cotangent = d_out.reshape(hidden_float.shape).astype(F32)
    block_out = (hidden_float + expert_sum).astype(BF).reshape(residual.shape)
    gained = d_normed * norm_gain
    d_norm_in = inv_rms * gained - hidden_float * inv_rms**3 * jnp.mean(
        gained * hidden_float, axis=-1, keepdims=True
    )
    d_hidden = (cotangent + d_norm_in).astype(BF).reshape(residual.shape)
    return (block_out, d_hidden, d_gate[None], d_up[None], d_down[None])


def solution(mesh):
    tok = P("frames", "expert", None)
    both = P(("frames", "expert"), None, None)
    return jax.shard_map(
        on_device,
        mesh=mesh,
        in_specs=(tok, tok, tok, tok, P(), P(), P(), P("expert", "frames", None, None), both, both, both, tok),
        out_specs=(tok, tok, both, both, both),
        check_vma=False,
    )
```

profile of v0, /device:TPU:0, one launch (start us, length us, event | category | flops | bytes accessed | tf_op | source)
XLA Modules:
  0.0 143.7 jit_solution(16195256173088986704)
XLA Ops:
  0.6 136.7 %shard_map.155 = (bf16[128,1152]{1,0:T(8,128)(2,1)}, f32[2,128,1152]{2,1,0:T(8,128)}, bf16[1152,512]{1,0:T(8,128)(2,1)}, bf16[1152,512]{1,0:T(8,128)(2,1)}, bf16[512,1152]{1,0:T(8,128)(2,1)}) custom-call(bf16[8,16,1152]{2,1,0:T(8,128)(2,1)} %bitcast.22, bf16[8,16,1152]{2,1,0:T(8,128)(2,1)} %bitcast.23, bf16[8,16,1152]{2,1,0:T(8,128)(2,1)} %bitcast.24, ...), custom_call_target="tpu_custom_call" | custom-call | tf_op jit(solution)/shard_map/pallas_call | solution.py:525
  137.4 6.3 %shard_map.156 = (bf16[128,1152]{1,0:T(8,128)(2,1)}, bf16[128,1152]{1,0:T(8,128)(2,1)}, f32[1152,512]{1,0:T(8,128)}, f32[1152,512]{1,0:T(8,128)}, f32[512,1152]{1,0:T(8,128)}) custom-call(bf16[128,1152]{1,0:T(8,128)(2,1)} %get-tuple-element.15.hidden_in, f32[2,128,1152]{2,1,0:T(8,128)} %get-tuple-element.16.sums_in, bf16[128,1152]{1,0:T(8,128)(2,1)} %bitcast.21, ...), custom_call_target="tpu_custom_call" | custom-call | tf_op jit(solution)/shard_map/pallas_call | solution.py:259
where the time goes:
time: 144 us
  Pallas kernels  143 us (99%)
    pallas_call x1, Pallas kernels, fused(): pl.pallas_call(functools.partial(fused_body, frames, depth), in_specs=[vm...  137 us
    pallas_call x1, Pallas kernels, tail(): pl.pallas_call(tail_body, in_specs=[ANY] * 3 + [vm] + [ANY] * 3, out_spec...  6.3 us

commit v1 on v0

--- a/solution.py
+++ b/solution.py
@@ -147,12 +147,12 @@
     )
 
 
-def each_peer(frames, f, fn):
+def each_peer(frames, f, fn, first=1, last=None):
     def step(o, carry):
         fn(o, lax.rem(f + o, frames), lax.rem(f + frames - o, frames))
         return carry
 
-    lax.fori_loop(1, frames, step, 0)
+    lax.fori_loop(first, last or frames, step, 0)
 
 
 def greet(frames, depth, f, z):
@@ -165,7 +165,7 @@
         pl.semaphore_signal(
             barrier, inc=1, device_id={"expert": lax.rem(z + o, depth)}, device_id_type=MESH
         )
-    pl.semaphore_wait(barrier, frames + depth - 2)
+    return lambda: pl.semaphore_wait(barrier, frames + depth - 2)
 
 
 def turn(k, z):
@@ -211,70 +211,49 @@
 
 
 def tail_body(
-    hidden_in, sums_in, d_out_in, gain, g0, g1, g2, block_out, d_hidden, o0, o1, o2,
-    hidden, sums, d_out, b0, b1, b2, w0, w1, w2, ls, ins, outs,
+    hidden, sums, d_out_in, gain, g0, g1, g2, block_out, d_hidden, o0, o1, o2, d_out, ls, outs,
 ):
-    small = [
-        pltpu.make_async_copy(src, dst, ls.at[i])
-        for i, (src, dst) in enumerate(((hidden_in, hidden), (sums_in, sums), (d_out_in, d_out)))
+    puts = [
+        pltpu.make_async_copy(src, dst, outs.at[i])
+        for i, (src, dst) in enumerate(((g0, o0), (g1, o1), (g2, o2)))
     ]
-    for c in small:
+    for c in puts:
         c.start()
-    steps = []
-    for i, (src, buf, wide, dst) in enumerate(
-        ((g0, b0, w0, o0), (g1, b1, w1, o1), (g2, b2, w2, o2))
-    ):
-        half = src.shape[0] // 2
-        for j in range(2):
-            at = pl.ds(j * half, half)
-            steps.append(
-                (
-                    pltpu.make_async_copy(src.at[at], buf.at[at], ins.at[i, j]),
-                    pltpu.make_async_copy(wide.at[at], dst.at[at], outs.at[i, j]),
-                    buf.at[at],
-                    wide.at[at],
-                )
-            )
-    for fetch, *_ in steps:
-        fetch.start()
-    for fetch, put, narrow, wide in steps:
-        fetch.wait()
-        wide[...] = narrow[...].astype(F32)
-        put.start()
-    for c in small:
-        c.wait()
+    load = pltpu.make_async_copy(d_out_in, d_out, ls)
+    load.start()
     hf = hidden[...].astype(F32)
     inv = lax.rsqrt(jnp.mean(hf * hf, axis=-1, keepdims=True) + 1e-06)
     block_out[...] = (hf + sums[0]).astype(BF)
     gained = sums[1] * gain[...].reshape(1, hf.shape[1])
     d_norm_in = inv * gained - hf * (inv * inv * inv) * jnp.mean(gained * hf, axis=-1, keepdims=True)
+    load.wait()
     d_hidden[...] = (d_out[...].astype(F32) + d_norm_in).astype(BF)
-    for _, put, *_ in steps:
-        put.wait()
+    for c in puts:
+        c.wait()
 
 
 def tail(hidden, sums, d_out, gain, grads):
     vm = pl.BlockSpec(memory_space=VM)
     dma = pltpu.SemaphoreType.DMA
+    kept = [pltpu.with_memory_space_constraint(t, VM) for t in (hidden, sums, *grads)]
     return pl.pallas_call(
         tail_body,
-        in_specs=[ANY] * 3 + [vm] + [ANY] * 3,
+        in_specs=[vm, vm, ANY, vm] + [vm] * 3,
         out_specs=[vm, vm, ANY, ANY, ANY],
         out_shape=[jax.ShapeDtypeStruct(hidden.shape, BF)] * 2
         + [jax.ShapeDtypeStruct(g.shape, F32) for g in grads],
-        scratch_shapes=[VM(t.shape, t.dtype) for t in (hidden, sums, d_out, *grads)]
-        + [VM(g.shape, F32) for g in grads]
-        + [dma((3,)), dma((3, 2)), dma((3, 2))],
-        compiler_params=pltpu.CompilerParams(vmem_limit_bytes=60 * 2**20),
-    )(hidden, sums, d_out, gain, *grads)
+        scratch_shapes=[VM(d_out.shape, d_out.dtype), dma(()), dma((3,))],
+        compiler_params=pltpu.CompilerParams(vmem_limit_bytes=32 * 2**20),
+    )(kept[0], kept[1], d_out, gain, *kept[2:])
 
 
 def fused_body(
-    frames, depth, q, k, v, d_out, routes, residual, w_out, gain, router, gate_in, up_in, down_in,
-    hidden, sums, gate_out, up_out, down_out,
-    d_gate, d_up, d_down, n_gate, n_up, n_down, proj, column, qkv, flat, acc, mix, att, place, pick, held_d, held, cot_slots, out_slots, x, cots,
-    gate, up, down, yr, back, part, swapped, merged, near, far,
-    qs, qr, ats, atr, ps, pr, ds, dr, zs, zr, cs, cr, xs, xr, ys, yr_sem, nsem, psem, fsem, ls,
+    frames, depth, q, k, v, d_out_in, routes_in, residual_in, w_out, gain_in, router_in, gate_in, up_in, down_in,
+    hidden, sums, d_gate, d_up, d_down,
+    routes, residual, gain, router, proj, column, qkv, flat, acc, mix, att, place, pick, d_out, d_across,
+    held, cot_slots, out_slots, x, cots,
+    gate, up, down, yr, back, part, passed, near, far,
+    qs, qr, ats, atr, ps, pr, dsem, zs, zr, cs, cr, es, er, xs, xr, ys, yr_sem, nsem, psem, fsem, ls,
 ):
     f, z = lax.axis_index("frames"), lax.axis_index("expert")
     _, positions, width = q.shape
@@ -284,17 +263,25 @@
     halves = depth // 2
     par = z % 2
     partner = z + 1 - 2 * par
+    across = z + halves - 2 * halves * (z // halves)
+    met = greet(frames, depth, f, z)
+    small = [
+        pltpu.make_async_copy(src, dst, ls.at[i])
+        for i, (src, dst) in enumerate(
+            ((routes_in, routes), (d_out_in, d_out), (router_in, router), (gain_in, gain), (residual_in, residual))
+        )
+    ]
+    own_qkv = [
+        pltpu.make_async_copy(t.at[f], qkv.at[i, f], ls.at[5 + i]) for i, t in enumerate((q, k, v))
+    ]
     loads = [
-        pltpu.make_async_copy(src, dst, ls.at[i])
+        pltpu.make_async_copy(src, dst, ls.at[8 + i])
         for i, (src, dst) in enumerate(((gate_in, gate), (up_in, up), (down_in, down)))
     ]
-    saves = [
-        pltpu.make_async_copy(src, dst, ls.at[3 + i])
-        for i, (src, dst) in enumerate(((n_gate, gate_out), (n_up, up_out), (n_down, down_out)))
-    ]
-    project = pltpu.make_async_copy(w_out, proj, ls.at[6])
-    project.start()
-    held_d[z] = d_out[...]
+    project = pltpu.make_async_copy(w_out, proj, ls.at[11])
+    for c in small + own_qkv + [project] + loads:
+        c.start()
+    small[0].wait()
     rows = lax.broadcasted_iota(jnp.int32, (halves * frames, tokens), 0)
     ids = (rows % frames) * halves + rows // frames
     hot = (routes[0:1, :] == ids) | (routes[1:2, :] == ids)
@@ -306,7 +293,17 @@
         preferred_element_type=F32,
     )
     place[z] = jnp.where(hot, before, -1.0).reshape(halves, frames, tokens)
-    greet(frames, depth, f, z)
+    slot = lax.broadcasted_iota(jnp.int32, (capacity, tokens), 0).astype(F32)
+
+    def choose(b):
+        at = place[b, z // halves]
+        for g in range(frames):
+            pick[b, g * capacity : (g + 1) * capacity, :] = jnp.where(
+                at[g : g + 1, :] == slot, 1.0, 0.0
+            ).astype(BF)
+
+    choose(z)
+    met()
 
     def exchange(fn, o, to, source):
         for i, t in enumerate((q, k, v)):
@@ -317,46 +314,61 @@
             place.at[source], place.at[source], ps.at[o], pr.at[o], expert=lax.rem(z + o, depth)
         )
 
+    def cross_copy():
+        return remote(d_out_in, d_across, dsem.at[0], dsem.at[1], expert=across)
+
+    each_peer(frames, f, lambda o, to, fr: exchange(lambda c: c.start(), o, to, f))
     for o in range(1, depth):
         place_copy(o, z).start()
-    each_peer(frames, f, lambda o, to, fr: exchange(lambda c: c.start(), o, to, f))
-    relay_d = Relay(depth, z, held_d, ds, dr)
-    relay_d.start(z)
-    for c in loads:
-        c.start()
+    cross_copy().start()
+
+    def mine(m):
+        return across if m else z
+
+    def cot_copy(m, o, to, source):
+        return remote(
+            cot_slots.at[m, to], cots.at[mine(m), source], cs.at[m, o], cr.at[m, o], frames=to
+        )
+
+    def send_cot(m):
+        cot_slots[m] = pick_rows(pick[mine(m)], (d_across if m else d_out)[...], frames)
+        each_peer(frames, f, lambda o, to, fr: cot_copy(m, o, to, f).start())
+        cots[mine(m), f] = cot_slots[m, f]
+
+    def share_copy(m, g):
+        piece = cots.at[mine(m), g]
+        return remote(piece, piece, es.at[m, g], er.at[m, g], expert=partner)
+
+    def share(m, first, last):
+        def step(o, to, fr):
+            cot_copy(m, o, to, fr).wait_recv()
+            share_copy(m, fr).start()
+
+        each_peer(frames, f, step, first, last)
+
+    def each_frame(fn):
+        def step(g, carry):
+            fn(g)
+            return carry
+
+        lax.fori_loop(0, frames, step, 0)
+
+    small[1].wait()
+    send_cot(0)
+    small[2].wait()
     expert_ids = lax.broadcasted_iota(jnp.int32, router.shape, 0)
     owned = expert_ids == (f * depth + z) // 2
     column[...] = jnp.sum(jnp.where(owned, router[...].astype(F32), 0.0), axis=0, keepdims=True)
-    for i, t in enumerate((q, k, v)):
-        qkv[i, f] = t[f]
     d_gate[...] = jnp.zeros(d_gate.shape, F32)
     d_up[...] = jnp.zeros(d_up.shape, F32)
     d_down[...] = jnp.zeros(d_down.shape, F32)
     for o in range(1, depth):
         place_copy(o, lax.rem(z + depth - o, depth)).wait_recv()
-    slot = lax.broadcasted_iota(jnp.int32, (capacity, tokens), 0).astype(F32)
-    for b in range(depth):
-        at = place[b, z // halves]
-        for g in range(frames):
-            pick[b, g * capacity : (g + 1) * capacity, :] = jnp.where(
-                at[g : g + 1, :] == slot, 1.0, 0.0
-            ).astype(BF)
-
-    def cot_copy(n, o, to, source):
-        b = turn(n, z)
-        return remote(cot_slots.at[b, to], cots.at[b, source], cs.at[n, o], cr.at[n, o], frames=to)
-
-    def send_cot(n):
-        b = turn(n, z)
-        if n:
-            relay_d.arrive(b)
-            relay_d.start(b)
-        cot_slots[b] = pick_rows(pick[b], held_d[b], frames)
-        each_peer(frames, f, lambda o, to, fr: cot_copy(n, o, to, f).start())
-        cots[b, f] = cot_slots[b, f]
-
+    for o in range(1, depth):
+        choose(lax.rem(z + o, depth))
+    for c in own_qkv:
+        c.wait()
     each_peer(frames, f, lambda o, to, fr: exchange(lambda c: c.wait_recv(), o, to, fr))
-    send_cot(0)
     for i in range(3):
         flat[i] = qkv[i].reshape(tokens, width)
     attend(flat.at[0], flat.at[1], flat.at[2], flat.at[3], acc, positions)
@@ -367,10 +379,14 @@
 
     each_peer(frames, f, lambda o, to, fr: home(o, to, f).start())
     att[f] = mix[f]
-    for n in range(1, depth):
-        send_cot(n)
+    cross_copy().wait_recv()
+    send_cot(1)
+    early = frames // 2
+    share_copy(0, f).start()
+    share(0, 1, early)
     each_peer(frames, f, lambda o, to, fr: home(o, to, fr).wait_recv())
-    project.wait()
+    for c in [project] + small[3:]:
+        c.wait()
     stream = residual[...].astype(F32) + jnp.dot(
         att[...].reshape(tokens, width), proj[...], preferred_element_type=F32
     )
@@ -389,7 +405,7 @@
 
     def send_slots(n):
         b = turn(n, z)
-        if not (isinstance(n, int) and n == 0):
+        if n:
             relay.arrive(b)
             relay.start(b)
         out_slots[b] = pick_rows(pick[b], held[b], frames)
@@ -400,10 +416,23 @@
         b = turn(n, z)
         return remote(yr.at[b, to], back.at[b, source], ys.at[n, o], yr_sem.at[n, o], frames=to)
 
+    def send_results(n):
+        b = turn(n, z)
+        each_peer(frames, f, lambda o, to, fr: result_copy(n, o, to, f).start())
+        back[b, f] = yr[b, f]
+
     def compute(n):
         b = turn(n, z)
         each_peer(frames, f, lambda o, to, fr: slot_copy(n, o, to, fr).wait_recv())
-        each_peer(frames, f, lambda o, to, fr: cot_copy(n, o, to, fr).wait_recv())
+
+        @pl.when(n == 1)
+        def _():
+            each_frame(lambda g: share_copy(0, g).wait_recv())
+
+        @pl.when((n > 1) & (b != across))
+        def _():
+            each_frame(lambda g: share_copy(1, g).wait_recv())
+
         xv = x[b].reshape(slots, width)
         cv = cots[b].reshape(slots, width)
         wr = column[...]
@@ -423,8 +452,11 @@
         d_logit = jnp.sum(cf * out, axis=-1, keepdims=True) * combine * (1.0 - combine)
         d_in = dot(dpg, gate[...], 1, 1) + dot(dpu, up[...], 1, 1)
         yr[b, :, 1] = (d_in + d_logit * wr).astype(BF).reshape(frames, capacity, width)
-        each_peer(frames, f, lambda o, to, fr: result_copy(n, o, to, f).start())
-        back[b, f] = yr[b, f]
+
+        @pl.when(n > 0)
+        def _():
+            send_results(n)
+
         d_gate[...] += dot(xv, dpg, 0, 0)
         d_up[...] += dot(xv, dpu, 0, 0)
         d_down[...] += dot(units, scaled, 0, 0)
@@ -435,79 +467,102 @@
         for i in range(2):
             yield dot(pick[b], back[b, :, i].reshape(slots, width), 0, 0)
 
-    def near_copy():
-        return remote(part.at[1], near, nsem.at[0], nsem.at[1], expert=partner)
-
-    def swap_copy(n):
-        return remote(part.at[n, 1 - par], swapped.at[n], psem.at[0, n], psem.at[1, n], expert=partner)
-
-    def far_copy(n):
-        return remote(merged.at[n], far.at[par], fsem.at[0, n], fsem.at[1, par], expert=turn(n, z))
+    outer = (z == 0) | (z == depth - 1)
+    opposite = jnp.where(z == halves, halves - 1, halves)
+
+    def inward(n, i):
+        return remote(
+            part.at[n, i], passed.at[n - 2, i], psem.at[0, n - 2, i], psem.at[1, n - 2, i], expert=partner
+        )
+
+    def over(n, i):
+        return remote(
+            part.at[n, i], far.at[n - 2, i], fsem.at[0, n - 2, i], fsem.at[1, n - 2, i], expert=opposite
+        )
+
+    def near_copy(i):
+        return remote(part.at[1, i], near.at[i], nsem.at[0, i], nsem.at[1, i], expert=partner)
 
     def collect(n):
         for i, total in enumerate(totals(n)):
             part[n, i] = total.astype(BF)
-
-        @pl.when(n == 1)
+            if n > 1:
+
+                @pl.when(outer)
+                def _():
+                    inward(n, i).start()
+
+    def forward(n):
+        @pl.when(jnp.logical_not(outer))
         def _():
-            near_copy().start()
-
-        @pl.when(n > 1)
-        def _():
-            swap_copy(n).start()
-
-    def forward(n):
-        swap_copy(n).wait_recv()
-        merged[n] = (part[n, par].astype(F32) + swapped[n].astype(F32)).astype(BF)
-        far_copy(n).start()
+            for i in range(2):
+                inward(n, i).wait_recv()
+                part[n, i] = (part[n, i].astype(F32) + passed[n - 2, i].astype(F32)).astype(BF)
+                over(n, i).start()
+
+    def hand_over():
+        for i in range(2):
+
+            @pl.when(jnp.logical_not(outer))
+            def _():
+                over(3, i).wait_recv()
+                part[1, i] = (part[1, i].astype(F32) + far[1, i].astype(F32)).astype(BF)
+
+            near_copy(i).start()
 
     for n in range(depth):
         send_slots(n)
+    share_copy(1, f).start()
+    share(1, 1, frames)
+    share(0, early, frames)
     for c in loads:
         c.wait()
 
-    def order(i):
-        return jnp.where(i < 2, i + 2, 3 - i)
-
     def step(i, carry):
-        compute(order(i))
-
-        @pl.when(i > 1)
-        def _():
-            forward(i)
-
-        @pl.when(i > 0)
-        def _():
-            collect(order(i - 1))
-
+        compute(jnp.where(i == 0, 0, jnp.where(i == depth - 1, 1, i + 1)))
         return carry
 
     lax.fori_loop(0, depth, step, 0)
-    for narrow, total in ((n_gate, d_gate), (n_up, d_up), (n_down, d_down)):
-        narrow[...] = total[...].astype(BF)
-    for c in saves:
-        c.start()
+    send_results(0)
+    for n in range(2, depth):
+        collect(n)
+        forward(n)
+    collect(1)
+    hand_over()
     own = list(totals(0))
-    near_copy().wait_recv()
+
     for i in range(2):
-        arrived = remote(merged.at[2], far.at[i], fsem.at[0, 2], fsem.at[1, i], expert=partner)
-        arrived.wait_recv()
-        sums[i] = own[i] + near[i].astype(F32) + far[i].astype(F32)
-    near_copy().wait_send()
-    for n in range(2, depth):
-        swap_copy(n).wait_send()
-        far_copy(n).wait_send()
+        near_copy(i).wait_recv()
+        sums[i] = own[i] + near[i].astype(F32)
+
+    @pl.when(jnp.logical_not(outer))
+    def _():
+        for i in range(2):
+            over(2, i).wait_recv()
+            sums[i] += far[0, i].astype(F32)
+
+    for i in range(2):
+        near_copy(i).wait_send()
+        for n in range(2, depth):
+
+            @pl.when(outer)
+            def _():
+                inward(n, i).wait_send()
+
+            @pl.when(jnp.logical_not(outer))
+            def _():
+                over(n, i).wait_send()
+
     for n in range(depth):
         each_peer(frames, f, lambda o, to, fr: slot_copy(n, o, to, f).wait_send())
         each_peer(frames, f, lambda o, to, fr: result_copy(n, o, to, f).wait_send())
     relay.finish()
-    for c in saves:
-        c.wait()
-    relay_d.finish()
+    cross_copy().wait_send()
     for o in range(1, depth):
         place_copy(o, z).wait_send()
-    for n in range(depth):
-        each_peer(frames, f, lambda o, to, fr: cot_copy(n, o, to, f).wait_send())
+    for m in range(2):
+        each_peer(frames, f, lambda o, to, fr: cot_copy(m, o, to, f).wait_send())
+        each_frame(lambda g: share_copy(m, g).wait_send())
     each_peer(frames, f, lambda o, to, fr: exchange(lambda c: c.wait_send(), o, to, f))
     each_peer(frames, f, lambda o, to, fr: home(o, to, f).wait_send())
 
@@ -517,6 +572,7 @@
     tokens = frames * positions
     dma = pltpu.SemaphoreType.DMA
     vm = pl.BlockSpec(memory_space=VM)
+    hbm = pl.BlockSpec(memory_space=pltpu.HBM)
     slots = (depth, frames, capacity, width)
     pair = (depth, frames, 2, capacity, width)
     blocks = (depth, tokens, width)
@@ -524,36 +580,37 @@
     two = (2, tokens, width)
     return pl.pallas_call(
         functools.partial(fused_body, frames, depth),
-        in_specs=[vm] * 6 + [ANY, vm, vm] + [ANY] * 3,
-        out_specs=[vm] * 2 + [ANY] * 3,
+        in_specs=[hbm] * 12,
+        out_specs=[vm] * 5,
         out_shape=[
-            jax.ShapeDtypeStruct((tokens, width), BF),
-            jax.ShapeDtypeStruct(two, F32),
-            jax.ShapeDtypeStruct(gate.shape, BF),
-            jax.ShapeDtypeStruct(up.shape, BF),
-            jax.ShapeDtypeStruct(down.shape, BF),
+            VM((tokens, width), BF),
+            VM(two, F32),
+            VM(gate.shape, F32),
+            VM(up.shape, F32),
+            VM(down.shape, F32),
         ],
         scratch_shapes=[
-            VM(gate.shape, F32), VM(up.shape, F32), VM(down.shape, F32),
-            VM(gate.shape, BF), VM(up.shape, BF), VM(down.shape, BF), VM(w_out.shape, BF), VM((1, width), F32),
+            VM(routes.shape, routes.dtype), VM(residual.shape, BF), VM(gain.shape, F32), VM(router.shape, BF),
+            VM(w_out.shape, BF), VM((1, width), F32),
             VM((3,) + chunked, BF), VM((4, tokens, width), BF), VM((tokens, width), F32),
             VM(chunked, BF), VM(chunked, BF),
             VM((depth, depth // 2, frames, tokens), F32),
             VM((depth, frames * capacity, tokens), BF),
-            VM(blocks, BF), VM(blocks, BF),
-            VM(slots, BF), VM(slots, BF), VM(slots, BF), VM(slots, BF),
+            VM((tokens, width), BF), VM((tokens, width), BF), VM(blocks, BF),
+            VM((2,) + slots[1:], BF), VM(slots, BF), VM(slots, BF), VM(slots, BF),
             VM(gate.shape, BF), VM(up.shape, BF), VM(down.shape, BF),
             VM(pair, BF), VM(pair, BF),
-            VM((depth,) + two, BF), VM(blocks, BF), VM(blocks, BF), VM(two, BF), VM(two, BF),
+            VM((depth,) + two, BF), VM((2,) + two, BF), VM(two, BF), VM((2,) + two, BF),
             dma((3, frames)), dma((3, frames)), dma((frames,)), dma((frames,)),
             dma((depth,)), dma((depth,)),
-            dma((2, depth)), dma((depth,)), dma((2, depth)), dma((depth,)),
-            dma((depth, frames)), dma((depth, frames)), dma((depth, frames)), dma((depth, frames)),
+            dma((2,)), dma((2, depth)), dma((depth,)),
+            dma((2, frames)), dma((2, frames)), dma((2, frames)), dma((2, frames)),
             dma((depth, frames)), dma((depth, frames)),
-            dma((2,)), dma((2, depth)), dma((2, depth)), dma((7,)),
+            dma((depth, frames)), dma((depth, frames)),
+            dma((2, 2)), dma((2, 2, 2)), dma((2, 2, 2)), dma((12,)),
         ],
         compiler_params=pltpu.CompilerParams(
-            collective_id=0, has_side_effects=True, vmem_limit_bytes=60 * 2**20
+            collective_id=0, has_side_effects=True, vmem_limit_bytes=52 * 2**20
         ),
     )(q, k, v, d_out, routes, residual, w_out, gain, router, gate, up, down)
 

time: 144 us -> 132 us (0.917); the launches traced: 144 us -> 130 us
  Pallas kernels: 143 us -> 130 us
    pallas_call x2, Pallas kernels: 143 us -> 130 us  [the longest x1 126 us: fused(): pl.pallas_call(functools.partial(fused_body, frames, depth), in_specs=[hb...]
where the time goes in v1:
time: 132 us; the launch traced here: 130 us
  Pallas kernels  130 us (98%)
    pallas_call x1, Pallas kernels, fused(): pl.pallas_call(functools.partial(fused_body, frames, depth), in_specs=[hb...  126 us
    pallas_call x1, Pallas kernels, tail(): pl.pallas_call(tail_body, in_specs=[vm, vm, ANY, vm] + [vm] * 3, out_spec...  3.81 us

profile of v1, /device:TPU:0, one launch (start us, length us, event | category | flops | bytes accessed | tf_op | source)
XLA Modules:
  0.0 130.2 jit_solution(4877859027159133203)
XLA Ops:
  0.6 0.0 copy-start
  0.6 0.0 copy-start.1
  0.7 125.7 %shard_map.155 = (bf16[128,1152]{1,0:T(8,128)(2,1)S(1)}, f32[2,128,1152]{2,1,0:T(8,128)S(1)}, f32[1152,512]{1,0:T(8,128)S(1)}, f32[1152,512]{1,0:T(8,128)S(1)}, f32[512,1152]{1,0:T(8,128)S(1)}) custom-call(bf16[8,16,1152]{2,1,0:T(8,128)(2,1)} %bitcast.22, bf16[8,16,1152]{2,1,0:T(8,128)(2,1)} %bitcast.23, bf16[8,16,1152]{2,1,0:T(8,128)(2,1)} %bitcast.24, ...), custom_call_target="tpu_custom_call" | custom-call | tf_op jit(solution)/shard_map/pallas_call | solution.py:581
  126.4 0.0 copy-done
  126.4 0.0 copy-done.1
  126.4 3.8 %shard_map.156 = (bf16[128,1152]{1,0:T(8,128)(2,1)}, bf16[128,1152]{1,0:T(8,128)(2,1)}, f32[1152,512]{1,0:T(8,128)}, f32[1152,512]{1,0:T(8,128)}, f32[512,1152]{1,0:T(8,128)}) custom-call(bf16[128,1152]{1,0:T(8,128)(2,1)S(1)} %get-tuple-element.15.hidden, f32[2,128,1152]{2,1,0:T(8,128)S(1)} %get-tuple-element.16.sums, bf16[128,1152]{1,0:T(8,128)(2,1)S(1)} %bitcast.18, ...), custom_call_target="tpu_custom_call" | custom-call | tf_op jit(solution)/shard_map/pallas_call | solution.py:239
Async XLA Ops:
  0.6 125.8 %copy-start = (bf16[1,128,1152]{2,1,0:T(8,128)(2,1)S(1)}, bf16[1,128,1152]{2,1,0:T(8,128)(2,1)}, u32[]{:S(2)}) copy-start(bf16[1,128,1152]{2,1,0:T(8,128)(2,1)} %param.23) | copy-start | bytes 884740
  0.6 125.8 %copy-start.1 = (f32[1152]{0:T(1024)S(1)}, f32[1152]{0:T(1024)}, u32[]{:S(2)}) copy-start(f32[1152]{0:T(1024)} %gain.1) | copy-start | bytes 13828

commit v2 on v1

--- a/solution.py
+++ b/solution.py
@@ -149,7 +149,11 @@
 
 def each_peer(frames, f, fn, first=1, last=None):
     def step(o, carry):
-        fn(o, lax.rem(f + o, frames), lax.rem(f + frames - o, frames))
+        peer, bit = 0, 1
+        while bit < frames:
+            low = (f // bit) % 2 + ((frames - o) // bit) % 2
+            peer, bit = peer + bit * (low % 2), bit * 2
+        fn(o, peer, peer)
         return carry
 
     lax.fori_loop(first, last or frames, step, 0)
@@ -412,14 +416,16 @@
         each_peer(frames, f, lambda o, to, fr: slot_copy(n, o, to, f).start())
         x[b, f] = out_slots[b, f]
 
-    def result_copy(n, o, to, source):
+    def result_copy(n, i, o, to, source):
         b = turn(n, z)
-        return remote(yr.at[b, to], back.at[b, source], ys.at[n, o], yr_sem.at[n, o], frames=to)
-
-    def send_results(n):
+        return remote(
+            yr.at[b, i, to], back.at[b, i, source], ys.at[n, i, o], yr_sem.at[n, i, o], frames=to
+        )
+
+    def send_results(n, i):
         b = turn(n, z)
-        each_peer(frames, f, lambda o, to, fr: result_copy(n, o, to, f).start())
-        back[b, f] = yr[b, f]
+        each_peer(frames, f, lambda o, to, fr: result_copy(n, i, o, to, f).start())
+        back[b, i, f] = yr[b, i, f]
 
     def compute(n):
         b = turn(n, z)
@@ -445,17 +451,22 @@
         act = pre_gate * sig
         units = (act * pre_up).astype(BF)
         out = dot(units, down[...], 1, 0).astype(BF).astype(F32)
-        yr[b, :, 0] = (combine * out).astype(BF).reshape(frames, capacity, width)
+        yr[b, 0] = (combine * out).astype(BF).reshape(frames, capacity, width)
+
+        @pl.when(n > 0)
+        def _():
+            send_results(n, 0)
+
         d_units = dot(scaled, down[...], 1, 1)
         dpg = (d_units * pre_up * (sig + act * (1.0 - sig))).astype(BF)
         dpu = (d_units * act).astype(BF)
         d_logit = jnp.sum(cf * out, axis=-1, keepdims=True) * combine * (1.0 - combine)
         d_in = dot(dpg, gate[...], 1, 1) + dot(dpu, up[...], 1, 1)
-        yr[b, :, 1] = (d_in + d_logit * wr).astype(BF).reshape(frames, capacity, width)
+        yr[b, 1] = (d_in + d_logit * wr).astype(BF).reshape(frames, capacity, width)
 
         @pl.when(n > 0)
         def _():
-            send_results(n)
+            send_results(n, 1)
 
         d_gate[...] += dot(xv, dpg, 0, 0)
         d_up[...] += dot(xv, dpu, 0, 0)
@@ -463,9 +474,9 @@
 
     def totals(n):
         b = turn(n, z)
-        each_peer(frames, f, lambda o, to, fr: result_copy(n, o, to, fr).wait_recv())
         for i in range(2):
-            yield dot(pick[b], back[b, :, i].reshape(slots, width), 0, 0)
+            each_peer(frames, f, lambda o, to, fr: result_copy(n, i, o, to, fr).wait_recv())
+            yield dot(pick[b], back[b, i].reshape(slots, width), 0, 0)
 
     outer = (z == 0) | (z == depth - 1)
     opposite = jnp.where(z == halves, halves - 1, halves)
@@ -486,11 +497,10 @@
     def collect(n):
         for i, total in enumerate(totals(n)):
             part[n, i] = total.astype(BF)
-            if n > 1:
-
-                @pl.when(outer)
-                def _():
-                    inward(n, i).start()
+
+            @pl.when(outer)
+            def _():
+                inward(n, i).start()
 
     def forward(n):
         @pl.when(jnp.logical_not(outer))
@@ -501,20 +511,37 @@
                 over(n, i).start()
 
     def hand_over():
-        for i in range(2):
+        for i, total in enumerate(totals(1)):
+
+            @pl.when(outer)
+            def _():
+                part[1, i] = total.astype(BF)
 
             @pl.when(jnp.logical_not(outer))
             def _():
                 over(3, i).wait_recv()
-                part[1, i] = (part[1, i].astype(F32) + far[1, i].astype(F32)).astype(BF)
+                part[1, i] = (total + far[1, i].astype(F32)).astype(BF)
 
             near_copy(i).start()
 
-    for n in range(depth):
+    def share_rest():
+        share_copy(1, f).start()
+        share(1, 1, frames)
+        share(0, early, frames)
+
+    send_slots(0)
+
+    @pl.when(outer)
+    def _():
+        share_rest()
+
+    for n in range(1, depth):
         send_slots(n)
-    share_copy(1, f).start()
-    share(1, 1, frames)
-    share(0, early, frames)
+
+    @pl.when(jnp.logical_not(outer))
+    def _():
+        share_rest()
+
     for c in loads:
         c.wait()
 
@@ -523,39 +550,10 @@
         return carry
 
     lax.fori_loop(0, depth, step, 0)
-    send_results(0)
-    for n in range(2, depth):
-        collect(n)
-        forward(n)
-    collect(1)
-    hand_over()
-    own = list(totals(0))
-
     for i in range(2):
-        near_copy(i).wait_recv()
-        sums[i] = own[i] + near[i].astype(F32)
-
-    @pl.when(jnp.logical_not(outer))
-    def _():
-        for i in range(2):
-            over(2, i).wait_recv()
-            sums[i] += far[0, i].astype(F32)
-
-    for i in range(2):
-        near_copy(i).wait_send()
-        for n in range(2, depth):
-
-            @pl.when(outer)
-            def _():
-                inward(n, i).wait_send()
-
-            @pl.when(jnp.logical_not(outer))
-            def _():
-                over(n, i).wait_send()
-
+        send_results(0, i)
     for n in range(depth):
         each_peer(frames, f, lambda o, to, fr: slot_copy(n, o, to, f).wait_send())
-        each_peer(frames, f, lambda o, to, fr: result_copy(n, o, to, f).wait_send())
     relay.finish()
     cross_copy().wait_send()
     for o in range(1, depth):
@@ -565,6 +563,37 @@
         each_frame(lambda g: share_copy(m, g).wait_send())
     each_peer(frames, f, lambda o, to, fr: exchange(lambda c: c.wait_send(), o, to, f))
     each_peer(frames, f, lambda o, to, fr: home(o, to, f).wait_send())
+    for n in range(2, depth):
+        collect(n)
+        forward(n)
+    hand_over()
+    own = list(totals(0))
+
+    for i in range(2):
+        near_copy(i).wait_recv()
+        sums[i] = own[i] + near[i].astype(F32)
+
+    @pl.when(jnp.logical_not(outer))
+    def _():
+        for i in range(2):
+            over(2, i).wait_recv()
+            sums[i] += far[0, i].astype(F32)
+
+    for i in range(2):
+        near_copy(i).wait_send()
+        for n in range(2, depth):
+
+            @pl.when(outer)
+            def _():
+                inward(n, i).wait_send()
+
+            @pl.when(jnp.logical_not(outer))
+            def _():
+                over(n, i).wait_send()
+
+    for n in range(depth):
+        for i in range(2):
+            each_peer(frames, f, lambda o, to, fr: result_copy(n, i, o, to, f).wait_send())
 
 
 def fused(q, k, v, d_out, routes, residual, w_out, gain, router, gate, up, down, depth, capacity):
@@ -574,7 +603,7 @@
     vm = pl.BlockSpec(memory_space=VM)
     hbm = pl.BlockSpec(memory_space=pltpu.HBM)
     slots = (depth, frames, capacity, width)
-    pair = (depth, frames, 2, capacity, width)
+    pair = (depth, 2, frames, capacity, width)
     blocks = (depth, tokens, width)
     chunked = (frames, positions, width)
     two = (2, tokens, width)
@@ -606,7 +635,7 @@
             dma((2,)), dma((2, depth)), dma((depth,)),
             dma((2, frames)), dma((2, frames)), dma((2, frames)), dma((2, frames)),
             dma((depth, frames)), dma((depth, frames)),
-            dma((depth, frames)), dma((depth, frames)),
+            dma((depth, 2, frames)), dma((depth, 2, frames)),
             dma((2, 2)), dma((2, 2, 2)), dma((2, 2, 2)), dma((12,)),
         ],
         compiler_params=pltpu.CompilerParams(
@@ -633,7 +662,7 @@
 
     own = (f * depth + z) // 2
     router = lax.dynamic_slice(w_router, (0, own), (width, 1)).reshape(1, width)
-    if positions % 16 == 0 and capacity % 16 == 0 and depth == 4:
+    if positions % 16 == 0 and capacity % 16 == 0 and depth == 4 and frames & (frames - 1) == 0:
         rows = d_out.reshape(tokens, width)
         hidden, sums, *grads = fused(
             *(t.reshape(frames, positions, width) for t in (queries, keys_in, values)),

time: 132 us -> 122 us (0.924); the launches traced: 130 us -> 122 us
  Pallas kernels: 130 us -> 121 us
    pallas_call x1, Pallas kernels: 126 us -> 118 us  [fused(): pl.pallas_call(functools.partial(fused_body, frames, depth), in_specs=[hb...]
where the time goes in v2:
time: 122 us
  Pallas kernels  121 us (99%)
    pallas_call x1, Pallas kernels, fused(): pl.pallas_call(functools.partial(fused_body, frames, depth), in_specs=[hb...  118 us
    pallas_call x1, Pallas kernels, tail(): pl.pallas_call(tail_body, in_specs=[vm, vm, ANY, vm] + [vm] * 3, out_spec...  3.81 us

profile of v2, /device:TPU:0, one launch (start us, length us, event | category | flops | bytes accessed | tf_op | source)
XLA Modules:
  0.0 122.1 jit_solution(4123046603052185698)
XLA Ops:
  0.6 0.0 copy-start
  0.6 0.0 copy-start.1
  0.7 117.6 %shard_map.155 = (bf16[128,1152]{1,0:T(8,128)(2,1)S(1)}, f32[2,128,1152]{2,1,0:T(8,128)S(1)}, f32[1152,512]{1,0:T(8,128)S(1)}, f32[1152,512]{1,0:T(8,128)S(1)}, f32[512,1152]{1,0:T(8,128)S(1)}) custom-call(bf16[8,16,1152]{2,1,0:T(8,128)(2,1)} %bitcast.22, bf16[8,16,1152]{2,1,0:T(8,128)(2,1)} %bitcast.23, bf16[8,16,1152]{2,1,0:T(8,128)(2,1)} %bitcast.24, ...), custom_call_target="tpu_custom_call" | custom-call | tf_op jit(solution)/shard_map/pallas_call | solution.py:610
  118.3 0.0 copy-done
  118.3 0.0 copy-done.1
  118.3 3.8 %shard_map.156 = (bf16[128,1152]{1,0:T(8,128)(2,1)}, bf16[128,1152]{1,0:T(8,128)(2,1)}, f32[1152,512]{1,0:T(8,128)}, f32[1152,512]{1,0:T(8,128)}, f32[512,1152]{1,0:T(8,128)}) custom-call(bf16[128,1152]{1,0:T(8,128)(2,1)S(1)} %get-tuple-element.15.hidden, f32[2,128,1152]{2,1,0:T(8,128)S(1)} %get-tuple-element.16.sums, bf16[128,1152]{1,0:T(8,128)(2,1)S(1)} %bitcast.18, ...), custom_call_target="tpu_custom_call" | custom-call | tf_op jit(solution)/shard_map/pallas_call | solution.py:243
Async XLA Ops:
  0.6 117.7 %copy-start = (bf16[1,128,1152]{2,1,0:T(8,128)(2,1)S(1)}, bf16[1,128,1152]{2,1,0:T(8,128)(2,1)}, u32[]{:S(2)}) copy-start(bf16[1,128,1152]{2,1,0:T(8,128)(2,1)} %param.23) | copy-start | bytes 884740
  0.6 117.7 %copy-start.1 = (f32[1152]{0:T(1024)S(1)}, f32[1152]{0:T(1024)}, u32[]{:S(2)}) copy-start(f32[1152]{0:T(1024)} %gain.1) | copy-start | bytes 13828

commit v3 on v2

--- a/solution.py
+++ b/solution.py
@@ -215,23 +215,27 @@
 
 
 def tail_body(
-    hidden, sums, d_out_in, gain, g0, g1, g2, block_out, d_hidden, o0, o1, o2, d_out, ls, outs,
+    hidden, sums, d_out_in, gain, g0, g1, g2, block_out, d_hidden, o0, o1, o2, d_out, first, second, ls, outs,
 ):
     puts = [
         pltpu.make_async_copy(src, dst, outs.at[i])
-        for i, (src, dst) in enumerate(((g0, o0), (g1, o1), (g2, o2)))
+        for i, (src, dst) in enumerate(
+            ((g0, o0), (g1, o1), (g2, o2), (first, block_out), (second, d_hidden))
+        )
     ]
-    for c in puts:
+    for c in puts[:3]:
         c.start()
     load = pltpu.make_async_copy(d_out_in, d_out, ls)
     load.start()
     hf = hidden[...].astype(F32)
     inv = lax.rsqrt(jnp.mean(hf * hf, axis=-1, keepdims=True) + 1e-06)
-    block_out[...] = (hf + sums[0]).astype(BF)
+    first[...] = (hf + sums[0]).astype(BF)
+    puts[3].start()
     gained = sums[1] * gain[...].reshape(1, hf.shape[1])
     d_norm_in = inv * gained - hf * (inv * inv * inv) * jnp.mean(gained * hf, axis=-1, keepdims=True)
     load.wait()
-    d_hidden[...] = (d_out[...].astype(F32) + d_norm_in).astype(BF)
+    second[...] = (d_out[...].astype(F32) + d_norm_in).astype(BF)
+    puts[4].start()
     for c in puts:
         c.wait()
 
@@ -243,10 +247,10 @@
     return pl.pallas_call(
         tail_body,
         in_specs=[vm, vm, ANY, vm] + [vm] * 3,
-        out_specs=[vm, vm, ANY, ANY, ANY],
+        out_specs=[ANY] * 5,
         out_shape=[jax.ShapeDtypeStruct(hidden.shape, BF)] * 2
         + [jax.ShapeDtypeStruct(g.shape, F32) for g in grads],
-        scratch_shapes=[VM(d_out.shape, d_out.dtype), dma(()), dma((3,))],
+        scratch_shapes=[VM(d_out.shape, BF)] * 3 + [dma(()), dma((5,))],
         compiler_params=pltpu.CompilerParams(vmem_limit_bytes=32 * 2**20),
     )(kept[0], kept[1], d_out, gain, *kept[2:])
 
@@ -546,6 +550,10 @@
         c.wait()
 
     def step(i, carry):
+        @pl.when(i == depth - 1)
+        def _():
+            collect(2)
+
         compute(jnp.where(i == 0, 0, jnp.where(i == depth - 1, 1, i + 1)))
         return carry
 
@@ -563,9 +571,9 @@
         each_frame(lambda g: share_copy(m, g).wait_send())
     each_peer(frames, f, lambda o, to, fr: exchange(lambda c: c.wait_send(), o, to, f))
     each_peer(frames, f, lambda o, to, fr: home(o, to, f).wait_send())
-    for n in range(2, depth):
-        collect(n)
-        forward(n)
+    forward(2)
+    collect(3)
+    forward(3)
     hand_over()
     own = list(totals(0))
 

time: 122 us -> 120 us (0.984)
  Pallas kernels: 121 us -> 119 us
    pallas_call x1, Pallas kernels: 118 us -> 116 us  [fused(): pl.pallas_call(functools.partial(fused_body, frames, depth), in_specs=[hb...]
where the time goes in v3:
time: 120 us; the launch traced here: 119 us
  Pallas kernels  119 us (99%)
    pallas_call x1, Pallas kernels, fused(): pl.pallas_call(functools.partial(fused_body, frames, depth), in_specs=[hb...  116 us
    pallas_call x1, Pallas kernels, tail(): pl.pallas_call(tail_body, in_specs=[vm, vm, ANY, vm] + [vm] * 3, out_spec...  3.12 us

profile of v3, /device:TPU:0, one launch (start us, length us, event | category | flops | bytes accessed | tf_op | source)
XLA Modules:
  0.0 119.5 jit_solution(15241519184035429272)
XLA Ops:
  0.6 0.0 copy-start
  0.6 0.0 copy-start.1
  0.7 115.7 %shard_map.155 = (bf16[128,1152]{1,0:T(8,128)(2,1)S(1)}, f32[2,128,1152]{2,1,0:T(8,128)S(1)}, f32[1152,512]{1,0:T(8,128)S(1)}, f32[1152,512]{1,0:T(8,128)S(1)}, f32[512,1152]{1,0:T(8,128)S(1)}) custom-call(bf16[8,16,1152]{2,1,0:T(8,128)(2,1)} %bitcast.22, bf16[8,16,1152]{2,1,0:T(8,128)(2,1)} %bitcast.23, bf16[8,16,1152]{2,1,0:T(8,128)(2,1)} %bitcast.24, ...), custom_call_target="tpu_custom_call" | custom-call | tf_op jit(solution)/shard_map/pallas_call | solution.py:618
  116.3 0.0 copy-done
  116.4 0.0 copy-done.1
  116.4 3.1 %shard_map.156 = (bf16[128,1152]{1,0:T(8,128)(2,1)}, bf16[128,1152]{1,0:T(8,128)(2,1)}, f32[1152,512]{1,0:T(8,128)}, f32[1152,512]{1,0:T(8,128)}, f32[512,1152]{1,0:T(8,128)}) custom-call(bf16[128,1152]{1,0:T(8,128)(2,1)S(1)} %get-tuple-element.15.hidden, f32[2,128,1152]{2,1,0:T(8,128)S(1)} %get-tuple-element.16.sums, bf16[128,1152]{1,0:T(8,128)(2,1)S(1)} %bitcast.18, ...), custom_call_target="tpu_custom_call" | custom-call | tf_op jit(solution)/shard_map/pallas_call | solution.py:247
Async XLA Ops:
  0.6 115.7 %copy-start = (bf16[1,128,1152]{2,1,0:T(8,128)(2,1)S(1)}, bf16[1,128,1152]{2,1,0:T(8,128)(2,1)}, u32[]{:S(2)}) copy-start(bf16[1,128,1152]{2,1,0:T(8,128)(2,1)} %param.23) | copy-start | bytes 884740
  0.6 115.7 %copy-start.1 = (f32[1152]{0:T(1024)S(1)}, f32[1152]{0:T(1024)}, u32[]{:S(2)}) copy-start(f32[1152]{0:T(1024)} %gain.1) | copy-start | bytes 13828

commit v4 on v3

--- a/solution.py
+++ b/solution.py
@@ -261,7 +261,7 @@
     routes, residual, gain, router, proj, column, qkv, flat, acc, mix, att, place, pick, d_out, d_across,
     held, cot_slots, out_slots, x, cots,
     gate, up, down, yr, back, part, passed, near, far,
-    qs, qr, ats, atr, ps, pr, dsem, zs, zr, cs, cr, es, er, xs, xr, ys, yr_sem, nsem, psem, fsem, ls,
+    qs, qr, ats, atr, ps, pr, dsem, zs, zr, cs, cr, es, er, hs, hr, xs, xr, ys, yr_sem, nsem, psem, fsem, ls,
 ):
     f, z = lax.axis_index("frames"), lax.axis_index("expert")
     _, positions, width = q.shape
@@ -272,6 +272,7 @@
     par = z % 2
     partner = z + 1 - 2 * par
     across = z + halves - 2 * halves * (z // halves)
+    cut = frames // 4 + 1
     met = greet(frames, depth, f, z)
     small = [
         pltpu.make_async_copy(src, dst, ls.at[i])
@@ -417,8 +418,15 @@
             relay.arrive(b)
             relay.start(b)
         out_slots[b] = pick_rows(pick[b], held[b], frames)
-        each_peer(frames, f, lambda o, to, fr: slot_copy(n, o, to, f).start())
+        each_peer(frames, f, lambda o, to, fr: slot_copy(n, o, to, f).start(), cut if n == 1 else 1)
         x[b, f] = out_slots[b, f]
+
+    def lend_copy(o, g):
+        piece = x.at[z, g]
+        return remote(piece, piece, hs.at[o], hr.at[o], expert=partner)
+
+    def lend():
+        each_peer(frames, f, lambda o, to, fr: lend_copy(o, fr).start(), 1, cut)
 
     def result_copy(n, i, o, to, source):
         b = turn(n, z)
@@ -433,11 +441,16 @@
 
     def compute(n):
         b = turn(n, z)
-        each_peer(frames, f, lambda o, to, fr: slot_copy(n, o, to, fr).wait_recv())
+        each_peer(frames, f, lambda o, to, fr: slot_copy(n, o, to, fr).wait_recv(), cut)
 
         @pl.when(n == 1)
         def _():
             each_frame(lambda g: share_copy(0, g).wait_recv())
+            each_peer(frames, f, lambda o, to, fr: lend_copy(o, fr).wait_recv(), 1, cut)
+
+        @pl.when(n != 1)
+        def _():
+            each_peer(frames, f, lambda o, to, fr: slot_copy(n, o, to, fr).wait_recv(), 1, cut)
 
         @pl.when((n > 1) & (b != across))
         def _():
@@ -476,9 +489,9 @@
         d_up[...] += dot(xv, dpu, 0, 0)
         d_down[...] += dot(units, scaled, 0, 0)
 
-    def totals(n):
+    def totals(n, arrays=(0, 1)):
         b = turn(n, z)
-        for i in range(2):
+        for i in arrays:
             each_peer(frames, f, lambda o, to, fr: result_copy(n, i, o, to, fr).wait_recv())
             yield dot(pick[b], back[b, i].reshape(slots, width), 0, 0)
 
@@ -498,21 +511,20 @@
     def near_copy(i):
         return remote(part.at[1, i], near.at[i], nsem.at[0, i], nsem.at[1, i], expert=partner)
 
-    def collect(n):
-        for i, total in enumerate(totals(n)):
-            part[n, i] = total.astype(BF)
-
-            @pl.when(outer)
-            def _():
-                inward(n, i).start()
-
-    def forward(n):
+    def collect(n, i):
+        (total,) = totals(n, (i,))
+        part[n, i] = total.astype(BF)
+
+        @pl.when(outer)
+        def _():
+            inward(n, i).start()
+
+    def forward(n, i):
         @pl.when(jnp.logical_not(outer))
         def _():
-            for i in range(2):
-                inward(n, i).wait_recv()
-                part[n, i] = (part[n, i].astype(F32) + passed[n - 2, i].astype(F32)).astype(BF)
-                over(n, i).start()
+            inward(n, i).wait_recv()
+            part[n, i] = (part[n, i].astype(F32) + passed[n - 2, i].astype(F32)).astype(BF)
+            over(n, i).start()
 
     def hand_over():
         for i, total in enumerate(totals(1)):
@@ -531,37 +543,46 @@
     def share_rest():
         share_copy(1, f).start()
         share(1, 1, frames)
-        share(0, early, frames)
+        each_peer(frames, f, lambda o, to, fr: share_copy(0, fr).start(), early)
 
     send_slots(0)
+    each_peer(frames, f, lambda o, to, fr: cot_copy(0, o, to, fr).wait_recv(), early)
 
     @pl.when(outer)
     def _():
         share_rest()
 
-    for n in range(1, depth):
+    for n in range(1, depth - 1):
         send_slots(n)
+    for c in loads:
+        c.wait()
+    compute(0)
+    send_slots(depth - 1)
 
     @pl.when(jnp.logical_not(outer))
     def _():
         share_rest()
 
-    for c in loads:
-        c.wait()
+    lend()
 
     def step(i, carry):
-        @pl.when(i == depth - 1)
-        def _():
-            collect(2)
-
-        compute(jnp.where(i == 0, 0, jnp.where(i == depth - 1, 1, i + 1)))
+        @pl.when(i == depth - 2)
+        def _():
+            collect(2, 0)
+            collect(2, 1)
+            forward(2, 0)
+
+        compute(jnp.where(i == depth - 2, 1, i + 2))
         return carry
 
-    lax.fori_loop(0, depth, step, 0)
+    lax.fori_loop(0, depth - 1, step, 0)
     for i in range(2):
         send_results(0, i)
     for n in range(depth):
-        each_peer(frames, f, lambda o, to, fr: slot_copy(n, o, to, f).wait_send())
+        each_peer(
+            frames, f, lambda o, to, fr: slot_copy(n, o, to, f).wait_send(), cut if n == 1 else 1
+        )
+    each_peer(frames, f, lambda o, to, fr: lend_copy(o, to).wait_send(), 1, cut)
     relay.finish()
     cross_copy().wait_send()
     for o in range(1, depth):
@@ -571,9 +592,10 @@
         each_frame(lambda g: share_copy(m, g).wait_send())
     each_peer(frames, f, lambda o, to, fr: exchange(lambda c: c.wait_send(), o, to, f))
     each_peer(frames, f, lambda o, to, fr: home(o, to, f).wait_send())
-    forward(2)
-    collect(3)
-    forward(3)
+    forward(2, 1)
+    for i in range(2):
+        collect(3, i)
+        forward(3, i)
     hand_over()
     own = list(totals(0))
 
@@ -642,6 +664,7 @@
             dma((depth,)), dma((depth,)),
             dma((2,)), dma((2, depth)), dma((depth,)),
             dma((2, frames)), dma((2, frames)), dma((2, frames)), dma((2, frames)),
+            dma((frames,)), dma((frames,)),
             dma((depth, frames)), dma((depth, frames)),
             dma((depth, 2, frames)), dma((depth, 2, frames)),
             dma((2, 2)), dma((2, 2, 2)), dma((2, 2, 2)), dma((12,)),

time: 120 us -> 119 us (level)
  Pallas kernels: 119 us -> 117 us
    pallas_call x1, Pallas kernels: 116 us -> 114 us  [fused(): pl.pallas_call(functools.partial(fused_body, frames, depth), in_specs=[hb...]
where the time goes in v4:
time: 119 us; the launch traced here: 118 us
  Pallas kernels  117 us (98%)
    pallas_call x1, Pallas kernels, fused(): pl.pallas_call(functools.partial(fused_body, frames, depth), in_specs=[hb...  114 us
    pallas_call x1, Pallas kernels, tail(): pl.pallas_call(tail_body, in_specs=[vm, vm, ANY, vm] + [vm] * 3, out_spec...  3.12 us

profile of v4, /device:TPU:0, one launch (start us, length us, event | category | flops | bytes accessed | tf_op | source)
XLA Modules:
  0.0 118.1 jit_solution(15915612642825831724)
XLA Ops:
  0.6 0.0 copy-start
  0.6 0.0 copy-start.1
  0.7 114.1 %shard_map.155 = (bf16[128,1152]{1,0:T(8,128)(2,1)S(1)}, f32[2,128,1152]{2,1,0:T(8,128)S(1)}, f32[1152,512]{1,0:T(8,128)S(1)}, f32[1152,512]{1,0:T(8,128)S(1)}, f32[512,1152]{1,0:T(8,128)S(1)}) custom-call(bf16[8,16,1152]{2,1,0:T(8,128)(2,1)} %bitcast.22, bf16[8,16,1152]{2,1,0:T(8,128)(2,1)} %bitcast.23, bf16[8,16,1152]{2,1,0:T(8,128)(2,1)} %bitcast.24, ...), custom_call_target="tpu_custom_call" | custom-call | tf_op jit(solution)/shard_map/pallas_call | solution.py:640
  114.8 0.0 copy-done
  114.8 0.0 copy-done.1
  114.8 3.1 %shard_map.156 = (bf16[128,1152]{1,0:T(8,128)(2,1)}, bf16[128,1152]{1,0:T(8,128)(2,1)}, f32[1152,512]{1,0:T(8,128)}, f32[1152,512]{1,0:T(8,128)}, f32[512,1152]{1,0:T(8,128)}) custom-call(bf16[128,1152]{1,0:T(8,128)(2,1)S(1)} %get-tuple-element.15.hidden, f32[2,128,1152]{2,1,0:T(8,128)S(1)} %get-tuple-element.16.sums, bf16[128,1152]{1,0:T(8,128)(2,1)S(1)} %bitcast.18, ...), custom_call_target="tpu_custom_call" | custom-call | tf_op jit(solution)/shard_map/pallas_call | solution.py:247
Async XLA Ops:
  0.6 114.2 %copy-start = (bf16[1,128,1152]{2,1,0:T(8,128)(2,1)S(1)}, bf16[1,128,1152]{2,1,0:T(8,128)(2,1)}, u32[]{:S(2)}) copy-start(bf16[1,128,1152]{2,1,0:T(8,128)(2,1)} %param.23) | copy-start | bytes 884740
  0.6 114.2 %copy-start.1 = (f32[1152]{0:T(1024)S(1)}, f32[1152]{0:T(1024)}, u32[]{:S(2)}) copy-start(f32[1152]{0:T(1024)} %gain.1) | copy-start | bytes 13828
